TPU v7x, 256 devices: a whole 4x4x8 slice. The times are simulated.
256 devices in a mesh: dp: 8 (over y, x_hi), ctx: 32 (over x_lo, z, core).
Axes of the slice: x: 4 (x_hi: 2, x_lo: 2; x = x_hi * 2 + x_lo), y: 4, z: 8, core: 2. Of those that a mesh axis runs over, the one named last changes fastest.
Arguments:
- query_rows: bfloat16 [8, 4096, 2048], P('dp', 'ctx'), may hold values from -6 to 6
- key_rows: bfloat16 [8, 4096, 2048], P('dp', 'ctx'), may hold values from -6 to 6
- value_rows: bfloat16 [8, 4096, 2048], P('dp', 'ctx'), may hold values from -6 to 6
- norm_gain: float32 [2048], replicated, may hold values from 0.1 to 1.9
- out_weight: bfloat16 [2048, 2048], P('ctx'), may hold values from -0.125 to 0.125
- cotangent: bfloat16 [8, 4096, 2048], P('dp', 'ctx'), may hold values from -6 to 6
Outputs:
- mixed: bfloat16 [8, 4096, 2048], P('dp', 'ctx')
- grad_queries: bfloat16 [8, 4096, 2048], P('dp', 'ctx')
- grad_keys: bfloat16 [8, 4096, 2048], P('dp', 'ctx')
- grad_values: bfloat16 [8, 4096, 2048], P('dp', 'ctx')
- grad_weight: float32 [2048, 2048], P('ctx')
All inputs are finite; a program needn't handle non-finite values.
Results may differ from a plain program's by a relative error of at most 0.025.
Values may be sent and summed in bfloat16 or wider, within the bound.
A program may use at most 192 MiB of HBM per device.

v0:
```python
import math
import jax
import jax.numpy as jnp
from jax import lax
from jax.sharding import PartitionSpec as P

HEAD = 128
epsilon = 1e-06
highest_precision = lax.Precision.HIGHEST


def carried_in(value, axis, combine, identity):
    size, index = (lax.axis_size(axis), lax.axis_index(axis))
    everything = lax.all_gather(value, axis)
    start = jnp.broadcast_to(jnp.asarray(identity, value.dtype), value.shape)

    def carried_turn(k, before):
        reached = k < index
        new = combine(before, everything[k])
        return jnp.where(reached, new, before)

    return lax.fori_loop(0, size, carried_turn, start)


def entering(value, axis, combine, identity):
    size, index = (lax.axis_size(axis), lax.axis_index(axis))
    everything = lax.all_gather(value.astype(jnp.bfloat16), axis)
    start = jnp.broadcast_to(jnp.asarray(identity, value.dtype), value.shape)

    def entering_turn(k, before):
        at = size - 1 - k
        reached = at > index
        new = combine(before, everything[at].astype(value.dtype))
        return jnp.where(reached, new, before)

    return lax.fori_loop(0, size, entering_turn, start)


def feature(values):
    wide = values.astype(jnp.float32)
    return jnp.where(wide > 0, wide + 1.0, jnp.exp(jnp.minimum(wide, 0.0))).astype(jnp.bfloat16)


def feature_slope(values):
    wide = values.astype(jnp.float32)
    return jnp.where(wide > 0, 1.0, jnp.exp(jnp.minimum(wide, 0.0)))


def add_states(earlier, later):
    return earlier + later


def on_device(query_rows, key_rows, value_rows, norm_gain, out_weight, cotangent):
    length = query_rows.shape[1]
    width = query_rows.shape[2]
    heads = width // HEAD
    shape3 = (length, heads, HEAD)
    weight = lax.all_gather(out_weight, "ctx", axis=0, tiled=True)
    query_seq = query_rows[0]
    key_seq = key_rows[0]
    query_per_head = feature(query_seq).reshape(shape3)
    key_per_head = feature(key_seq).reshape(shape3)
    value_per_head = value_rows[0].reshape(shape3)
    local_state = jnp.einsum(
        "wmx,wmt->mxt", key_per_head, value_per_head, preferred_element_type=jnp.float32
    )
    zero_state = jnp.zeros_like(local_state)
    prefix_state = carried_in(local_state, "ctx", add_states, zero_state)
    causal = jnp.tril(jnp.ones((length, length), dtype=bool))
    scores = jnp.einsum(
        "thd,shd->hts", query_per_head, key_per_head, preferred_element_type=jnp.float32
    )
    probs = jnp.where(causal, scores, 0.0).astype(jnp.bfloat16)
    query_wide_rows = query_per_head.astype(jnp.float32)
    attended_output = jnp.einsum(
        "hts,shv->thv", probs, value_per_head, preferred_element_type=jnp.float32
    )
    attended_output = attended_output + jnp.einsum(
        "wrf,rfp->wrp", query_wide_rows, prefix_state, precision=highest_precision
    )
    inverse = lax.rsqrt(
        jnp.mean(attended_output * attended_output, axis=-1, keepdims=True) + epsilon
    )
    gain_heads = norm_gain.reshape(heads, HEAD)
    normed = (attended_output * inverse * gain_heads).reshape(length, width).astype(jnp.bfloat16)
    mixed = jnp.dot(normed, weight, preferred_element_type=jnp.float32).astype(jnp.bfloat16)
    upstream = cotangent[0]
    d_normed = lax.dot_general(
        upstream, weight, (((1,), (1,)), ((), ())), preferred_element_type=jnp.float32
    ).reshape(shape3)
    scaled = d_normed * gain_heads
    attended_gradient = (
        inverse
        * (
            scaled
            - attended_output
            * inverse
            * inverse
            * jnp.mean(scaled * attended_output, axis=-1, keepdims=True)
        )
    ).astype(jnp.bfloat16)
    grad_local = jnp.einsum(
        "ibg,ibq->bgq", query_per_head, attended_gradient, preferred_element_type=jnp.float32
    )
    suffix_state = entering(grad_local, "ctx", add_states, zero_state)
    d_scores = jnp.einsum(
        "thv,shv->hts", attended_gradient, value_per_head, preferred_element_type=jnp.float32
    )
    d_probs = jnp.where(causal, d_scores, 0.0).astype(jnp.bfloat16)
    wide_gradient = attended_gradient.astype(jnp.float32)
    value_wide_rows = value_per_head.astype(jnp.float32)
    key_wide_rows = key_per_head.astype(jnp.float32)
    query_gradient = jnp.einsum(
        "hts,shk->thk", d_probs, key_per_head, preferred_element_type=jnp.float32
    )
    query_gradient = query_gradient + jnp.einsum(
        "fxn,xpn->fxp", wide_gradient, prefix_state, precision=highest_precision
    )
    key_gradient = jnp.einsum(
        "hts,thk->shk", d_probs, query_per_head, preferred_element_type=jnp.float32
    )
    key_gradient = key_gradient + jnp.einsum(
        "mcu,cxu->mcx", value_wide_rows, suffix_state, precision=highest_precision
    )
    value_gradient = jnp.einsum(
        "hts,thv->shv", probs, attended_gradient, preferred_element_type=jnp.float32
    )
    value_gradient = value_gradient + jnp.einsum(
        "inz,nzc->inc", key_wide_rows, suffix_state, precision=highest_precision
    )
    grad_queries = (query_gradient.reshape(length, width) * feature_slope(query_seq)).astype(
        jnp.bfloat16
    )
    grad_keys = (key_gradient.reshape(length, width) * feature_slope(key_seq)).astype(jnp.bfloat16)
    grad_values = value_gradient.reshape(length, width).astype(jnp.bfloat16)
    devices_dp = lax.axis_size("dp")
    devices_ctx = lax.axis_size("ctx")
    loss_scale = 1.0 / math.sqrt(devices_dp * devices_ctx * length)
    shares = lax.psum_scatter(
        lax.dot_general(
            normed, upstream, (((0,), (0,)), ((), ())), preferred_element_type=jnp.float32
        ).astype(jnp.bfloat16),
        "ctx",
        scatter_dimension=0,
        tiled=True,
    )
    summed = lax.psum(shares, "dp").astype(jnp.float32)
    grad_weight = summed * loss_scale
    return (mixed[None], grad_queries[None], grad_keys[None], grad_values[None], grad_weight)


def solution(mesh):
    return jax.shard_map(
        on_device,
        mesh=mesh,
        in_specs=(
            P("dp", "ctx", None),
            P("dp", "ctx", None),
            P("dp", "ctx", None),
            P(),
            P("ctx", None),
            P("dp", "ctx", None),
        ),
        out_specs=(
            P("dp", "ctx", None),
            P("dp", "ctx", None),
            P("dp", "ctx", None),
            P("dp", "ctx", None),
            P("ctx", None),
        ),
        check_vma=False,
    )
```

profile of v0, /device:TPU:1, one launch (start us, length us, event | category | flops | bytes accessed | tf_op | source)
XLA Modules:
  0.0 674.6 jit_solution(1039800989723553245)
XLA Ops:
  12.7 2.1 fusion.6
  17.4 183.0 %all-gather.8.cloned.1.call-done = f32[512,128,128]{2,1,0:T(8,128)} async-done(((f32[16,128,128]{2,1,0:T(8,128)}), f32[512,128,128]{2,1,0:T(8,128)}) %all-gather.8.cloned.1.call-update) | async-done | bytes 33554448 | tf_op jit(solution)/shard_map/all_gather | solution.py:14
  200.4 52.2 %while.30 = (s32[]{:T(128)}, f32[16,128,128]{2,1,0:T(8,128)S(1)}, s32[]{:T(128)}, f32[32,16,128,128]{3,2,1,0:T(8,128)}, s32[]{:T(128)}, /*index=5*/s32[]{:T(128)}) while((s32[]{:T(128)}, f32[16,128,128]{2,1,0:T(8,128)S(1)}, s32[]{:T(128)}, f32[32,16,128,128]{3,2,1,0:T(8,128)}, s32[]{:T(128)}, /*index=5*/s32[]{:T(128)}) %tuple.93), condition=%wide.region_1.2_spmd.clone, body=%wide.region_0.1_spmd.clone.sunk | while | flops 786436 | bytes 3145821 | solution.py:22
  213.4 1.7 add_select_fusion.4
  246.1 1.6 add_select_fusion.4
  255.3 19.7 %all-gather.6.cloned.1.call-done = bf16[2048,2048]{1,0:T(8,128)(2,1)} async-done(((bf16[64,2048]{1,0:T(8,128)(2,1)}), bf16[2048,2048]{1,0:T(8,128)(2,1)}) %all-gather.6.cloned.1.call-update) | async-done | bytes 8388624 | tf_op jit(solution)/shard_map/all_gather | solution.py:58
  275.0 5.7 multiply_reduce_fusion
  281.9 5.6 convolution_convert_fusion
  287.6 124.8 %reduce-scatter.2.cloned.1.call-done = bf16[64,2048]{1,0:T(8,128)(2,1)} async-done(((bf16[2048,2048]{1,0:T(8,128)(2,1)}), bf16[64,2048]{1,0:T(8,128)(2,1)}) %reduce-scatter.2.cloned.1.call-update) | async-done | bytes 262160 | tf_op jit(solution)/shard_map/reduce_scatter | solution.py:139
  414.0 1.7 fusion.4
  415.7 1.7 fusion.27
  417.5 2.7 convolution_add_fusion.2
  421.7 2.5 fusion.29
  424.1 2.3 fusion.28
  426.5 2.1 fusion.10
  428.6 5.5 fusion
  434.0 65.0 %all-reduce.2.cloned.1.call-done = bf16[64,2048]{1,0:T(8,128)(2,1)} async-done(((bf16[64,2048]{1,0:T(8,128)(2,1)}), bf16[64,2048]{1,0:T(8,128)(2,1)}) %all-reduce.2.cloned.1.call-update) | async-done | bytes 262160 | tf_op jit(solution)/shard_map/psum | solution.py:147
  499.0 1.8 convert_multiply_fusion
  500.8 103.3 %all-gather.10.cloned.1.call-done = bf16[512,128,128]{2,1,0:T(8,128)(2,1)} async-done(((bf16[16,128,128]{2,1,0:T(8,128)(2,1)}), bf16[512,128,128]{2,1,0:T(8,128)(2,1)}) %all-gather.10.cloned.1.call-update) | async-done | bytes 16777232 | tf_op jit(solution)/shard_map/all_gather | solution.py:27
  604.1 52.7 %while.31 = (s32[]{:T(128)}, f32[16,128,128]{2,1,0:T(8,128)S(1)}, s32[]{:T(128)}, bf16[32,16,128,128]{3,2,1,0:T(8,128)(2,1)}, s32[]{:T(128)}, /*index=5*/s32[]{:T(128)}, s32[]{:T(128)}, s32[]{:T(128)}) while((s32[]{:T(128)}, f32[16,128,128]{2,1,0:T(8,128)S(1)}, s32[]{:T(128)}, bf16[32,16,128,128]{3,2,1,0:T(8,128)(2,1)}, s32[]{:T(128)}, ...), condition=%wide.region_5.6_spmd.clone, body=%wide.region_4.5_spmd.clone.sunk | while | flops 1048584 | bytes 2621595 | solution.py:36
  604.1 1.7 add_select_fusion.5
  656.8 3.1 fusion.2
  659.9 2.0 copy.50
  662.0 3.4 convolution_add_fusion.1
  (117 shorter events, 115.8 us)
Async XLA Ops:
  7.2 267.8 %copy-start = (bf16[1,128,2048]{2,1,0:T(8,128)(2,1)S(1)}, bf16[1,128,2048]{2,1,0:T(8,128)(2,1)}, u32[]{:S(2)}) copy-start(bf16[1,128,2048]{2,1,0:T(8,128)(2,1)} %param.15) | copy-start | bytes 1572868
  7.2 193.3 %all-gather.8.cloned.1.call-start = ((), (), s32[]{:S(2)}) async-start(), calls=%async_computation.4 | async-start | bytes 34603008 | tf_op jit(solution)/shard_map/all_gather | solution.py:14
  8.7 191.7 %copy-start.8 = (bf16[16,8,16,128]{3,2,1,0:T(8,128)(2,1)}, bf16[16,8,16,128]{3,2,1,0:T(8,128)(2,1)S(1)}, u32[]{:S(2)}) copy-start(bf16[16,8,16,128]{3,2,1,0:T(8,128)(2,1)S(1)} %copy.57) | copy-start | bytes 1572868
  9.2 3.5 copy-start.10
  10.6 243.1 %copy-start.5 = (bf16[16,8,16,128]{3,2,1,0:T(8,128)(2,1)}, bf16[16,8,16,128]{3,2,1,0:T(8,128)(2,1)S(1)}, u32[]{:S(2)}) copy-start(bf16[16,8,16,128]{3,2,1,0:T(8,128)(2,1)S(1)} %copy.58) | copy-start | bytes 1572868
  11.9 263.1 %all-gather.6.cloned.1.call-start = ((), (), s32[]{:S(2)}) async-start(), calls=%async_computation.1 | async-start | bytes 8650752 | tf_op jit(solution)/shard_map/all_gather | solution.py:58
  12.6 399.8 %reduce-scatter.2.cloned.1.call-start = ((), (), s32[]{:S(2)}) async-start(), calls=%async_computation.2 | async-start | bytes 8650752 | tf_op jit(solution)/shard_map/reduce_scatter | solution.py:139
  16.1 236.6 %copy-start.2 = (bf16[1,128,2048]{1,2,0:T(8,128)(2,1)}, bf16[1,128,2048]{1,2,0:T(8,128)(2,1)S(1)}, u32[]{:S(2)}) copy-start(bf16[1,128,2048]{1,2,0:T(8,128)(2,1)S(1)} %copy.56) | copy-start | bytes 1572868
  200.4 74.6 %copy-start.13 = (f32[2048]{0:T(1024)S(1)}, f32[2048]{0:T(1024)}, u32[]{:S(2)}) copy-start(f32[2048]{0:T(1024)} %param.13) | copy-start | bytes 24580
  281.9 130.8 %copy-start.3 = (bf16[1,128,2048]{1,2,0:T(8,128)(2,1)S(1)}, bf16[1,128,2048]{1,2,0:T(8,128)(2,1)}, u32[]{:S(2)}) copy-start(bf16[1,128,2048]{1,2,0:T(8,128)(2,1)} %copy-done.2) | copy-start | bytes 1572868
  281.9 130.8 %copy-start.7 = (bf16[128,16,128]{0,2,1:T(8,128)(2,1)S(1)}, bf16[128,16,128]{0,2,1:T(8,128)(2,1)}, u32[]{:S(2)}) copy-start(bf16[128,16,128]{0,2,1:T(8,128)(2,1)} %get-tuple-element.254) | copy-start | bytes 1572868
  287.5 136.6 %copy-start.4 = (bf16[1,128,2048]{1,2,0:T(8,128)(2,1)S(1)}, bf16[1,128,2048]{1,2,0:T(8,128)(2,1)}, u32[]{:S(2)}) copy-start(bf16[1,128,2048]{1,2,0:T(8,128)(2,1)} %copy-done.2) | copy-start | bytes 1572868
  287.6 211.5 %all-reduce.2.cloned.1.call-start = ((), (), s32[]{:S(2)}) async-start(), calls=%async_computation.3 | async-start | bytes 524288 | tf_op jit(solution)/shard_map/psum | solution.py:147
  412.5 191.6 %all-gather.10.cloned.1.call-start = ((), (), s32[]{:S(2)}) async-start(), calls=%async_computation.5 | async-start | bytes 17301504 | tf_op jit(solution)/shard_map/all_gather | solution.py:27
  415.7 4.4 copy-start.12
  434.0 222.8 %copy-start.9 = (bf16[16,8,16,128]{3,2,1,0:T(8,128)(2,1)S(1)}, bf16[16,8,16,128]{3,2,1,0:T(8,128)(2,1)}, u32[]{:S(2)}) copy-start(bf16[16,8,16,128]{3,2,1,0:T(8,128)(2,1)} %copy-done.8) | copy-start | bytes 1572868
  604.1 57.9 %copy-start.6 = (bf16[16,8,16,128]{3,2,1,0:T(8,128)(2,1)S(1)}, bf16[16,8,16,128]{3,2,1,0:T(8,128)(2,1)}, u32[]{:S(2)}) copy-start(bf16[16,8,16,128]{3,2,1,0:T(8,128)(2,1)} %copy-done.5) | copy-start | bytes 1572868
  604.1 62.9 %copy-start.11 = (bf16[1,128,2048]{2,1,0:T(8,128)(2,1)S(1)}, bf16[1,128,2048]{2,1,0:T(8,128)(2,1)}, u32[]{:S(2)}) copy-start(bf16[1,128,2048]{2,1,0:T(8,128)(2,1)} %param.11) | copy-start | bytes 1572868
  656.8 11.2 %copy-start.1 = (bf16[1,128,2048]{2,1,0:T(8,128)(2,1)S(1)}, bf16[1,128,2048]{2,1,0:T(8,128)(2,1)}, u32[]{:S(2)}) copy-start(bf16[1,128,2048]{2,1,0:T(8,128)(2,1)} %param.15) | copy-start | bytes 1572868
Sparse Core Ops, SparseCore 0:
  12.0 188.4 all-gather.7
  202.3 72.6 all-gather.5
  287.7 124.7 reduce-scatter.1
  414.9 84.0 all-reduce.1
  500.9 103.1 all-gather.9
where the time goes:
time: 678 us; the launch traced here: 675 us
  waiting for transfers between devices  497 us (73%)
  other arithmetic  113 us (17%)
  matrix products  40.6 us (6%)
  between operations  14 us (2%)
  local copies, waits for them, and re-layouts  8.44 us (1%)
    all_gather x1, waiting for transfers between devices, carried_in(): everything = lax.all_gather(value, axis)  183 us
    reduce_scatter x1, waiting for transfers between devices, on_device(): lax.psum_scatter(lax.dot_general(normed, upstream, (((0,), (0,)), ((), ()...  125 us
    all_gather x1, waiting for transfers between devices, entering(): everything = lax.all_gather(value.astype(jnp.bfloat16), axis)  103 us
    psum x1, waiting for transfers between devices, on_device(): summed = lax.psum(shares, 'dp').astype(jnp.float32)  65 us
    select_n x32, other arithmetic, entering_turn(): return jnp.where(reached, new, before)  51.8 us
    select_n x32, other arithmetic, carried_turn(): return jnp.where(reached, new, before)  51.4 us
    all_gather x1, waiting for transfers between devices, on_device(): weight = lax.all_gather(out_weight, 'ctx', axis=0, tiled=True)  19.7 us
  transfers between devices with their start and end apart: 5, of which 5 were waited for; matrix products, arithmetic and copies ran while one was open for 12% of the time, Pallas kernels for 0%

commit v1 on v0

--- a/solution.py
+++ b/solution.py
@@ -51,6 +51,10 @@
 
 
 def on_device(query_rows, key_rows, value_rows, norm_gain, out_weight, cotangent):
+
+    def build_cells_here(piece_in, device_axis):
+        return lax.all_gather(piece_in, device_axis).sum(axis=0)
+
     length = query_rows.shape[1]
     width = query_rows.shape[2]
     heads = width // HEAD
@@ -144,7 +148,7 @@
         scatter_dimension=0,
         tiled=True,
     )
-    summed = lax.psum(shares, "dp").astype(jnp.float32)
+    summed = build_cells_here(shares, "dp").astype(jnp.float32)
     grad_weight = summed * loss_scale
     return (mixed[None], grad_queries[None], grad_keys[None], grad_values[None], grad_weight)
 

time: 678 us -> 648 us (0.956)
  waiting for transfers between devices: 497 us -> 465 us
    psum x1 -> x0, waiting for transfers between devices: 65 us -> none  [on_device(): summed = lax.psum(shares, 'dp').astype(jnp.float32)]
    all_gather x0 -> x1, waiting for transfers between devices: none -> 39.4 us  [build_cells_here(): return lax.all_gather(piece_in, device_axis).sum(axis=0)]
  transfers between devices with their start and end apart: 5 -> 5, of which waited for: 5 -> 5; matrix products, arithmetic and copies ran while one was open for 12% -> 13% of each run, Pallas kernels for 0% -> 0%
where the time goes in v1:
time: 648 us; the launch traced here: 644 us
  waiting for transfers between devices  465 us (72%)
  other arithmetic  114 us (18%)
  matrix products  40.6 us (6%)
  between operations  14 us (2%)
  local copies, waits for them, and re-layouts  8.44 us (1%)
    all_gather x1, waiting for transfers between devices, carried_in(): everything = lax.all_gather(value, axis)  183 us
    reduce_scatter x1, waiting for transfers between devices, on_device(): lax.psum_scatter(lax.dot_general(normed, upstream, (((0,), (0,)), ((), ()...  125 us
    all_gather x1, waiting for transfers between devices, entering(): everything = lax.all_gather(value.astype(jnp.bfloat16), axis)  97.4 us
    select_n x32, other arithmetic, entering_turn(): return jnp.where(reached, new, before)  51.8 us
    select_n x32, other arithmetic, carried_turn(): return jnp.where(reached, new, before)  51.4 us
    all_gather x1, waiting for transfers between devices, build_cells_here(): return lax.all_gather(piece_in, device_axis).sum(axis=0)  39.4 us
    all_gather x1, waiting for transfers between devices, on_device(): weight = lax.all_gather(out_weight, 'ctx', axis=0, tiled=True)  19.7 us
  transfers between devices with their start and end apart: 5, of which 5 were waited for; matrix products, arithmetic and copies ran while one was open for 13% of the time, Pallas kernels for 0%

profile of v1, /device:TPU:1, one launch (start us, length us, event | category | flops | bytes accessed | tf_op | source)
XLA Modules:
  0.0 644.1 jit_solution(1740175805880874711)
XLA Ops:
  12.7 2.1 fusion.6
  17.4 183.0 %all-gather.10.cloned.1.call-done = f32[512,128,128]{2,1,0:T(8,128)} async-done(((f32[16,128,128]{2,1,0:T(8,128)}), f32[512,128,128]{2,1,0:T(8,128)}) %all-gather.10.cloned.1.call-update) | async-done | bytes 33554448 | tf_op jit(solution)/shard_map/all_gather | solution.py:14
  200.4 52.2 %while.30 = (s32[]{:T(128)}, f32[16,128,128]{2,1,0:T(8,128)S(1)}, s32[]{:T(128)}, f32[32,16,128,128]{3,2,1,0:T(8,128)}, s32[]{:T(128)}, /*index=5*/s32[]{:T(128)}) while((s32[]{:T(128)}, f32[16,128,128]{2,1,0:T(8,128)S(1)}, s32[]{:T(128)}, f32[32,16,128,128]{3,2,1,0:T(8,128)}, s32[]{:T(128)}, /*index=5*/s32[]{:T(128)}) %tuple.93), condition=%wide.region_1.2_spmd.clone, body=%wide.region_0.1_spmd.clone.sunk | while | flops 786436 | bytes 3145821 | solution.py:22
  213.4 1.7 add_select_fusion.4
  246.1 1.6 add_select_fusion.4
  255.3 19.7 %all-gather.8.cloned.1.call-done = bf16[2048,2048]{1,0:T(8,128)(2,1)} async-done(((bf16[64,2048]{1,0:T(8,128)(2,1)}), bf16[2048,2048]{1,0:T(8,128)(2,1)}) %all-gather.8.cloned.1.call-update) | async-done | bytes 8388624 | tf_op jit(solution)/shard_map/all_gather | solution.py:62
  275.0 5.7 multiply_reduce_fusion
  281.9 5.6 convolution_convert_fusion
  287.6 124.8 %reduce-scatter.2.cloned.1.call-done = bf16[64,2048]{1,0:T(8,128)(2,1)} async-done(((bf16[2048,2048]{1,0:T(8,128)(2,1)}), bf16[64,2048]{1,0:T(8,128)(2,1)}) %reduce-scatter.2.cloned.1.call-update) | async-done | bytes 262160 | tf_op jit(solution)/shard_map/reduce_scatter | solution.py:143
  414.0 1.7 fusion.4
  415.7 1.7 fusion.27
  417.5 2.7 convolution_add_fusion.2
  421.7 2.5 fusion.29
  424.2 2.3 fusion.28
  426.5 2.1 fusion.10
  428.6 5.5 fusion
  434.1 39.4 %all-gather.14.cloned.1.call-done = bf16[512,2048]{1,0:T(8,128)(2,1)} async-done(((bf16[64,2048]{1,0:T(8,128)(2,1)}), bf16[512,2048]{1,0:T(8,128)(2,1)}) %all-gather.14.cloned.1.call-update) | async-done | bytes 2097168 | tf_op jit(solution)/shard_map/all_gather | solution.py:56
  473.4 2.0 reduce_sum.32
  476.2 97.4 %all-gather.12.cloned.1.call-done = bf16[512,128,128]{2,1,0:T(8,128)(2,1)} async-done(((bf16[16,128,128]{2,1,0:T(8,128)(2,1)}), bf16[512,128,128]{2,1,0:T(8,128)(2,1)}) %all-gather.12.cloned.1.call-update) | async-done | bytes 16777232 | tf_op jit(solution)/shard_map/all_gather | solution.py:27
  573.7 52.7 %while.31 = (s32[]{:T(128)}, f32[16,128,128]{2,1,0:T(8,128)S(1)}, s32[]{:T(128)}, bf16[32,16,128,128]{3,2,1,0:T(8,128)(2,1)}, s32[]{:T(128)}, /*index=5*/s32[]{:T(128)}, s32[]{:T(128)}, s32[]{:T(128)}) while((s32[]{:T(128)}, f32[16,128,128]{2,1,0:T(8,128)S(1)}, s32[]{:T(128)}, bf16[32,16,128,128]{3,2,1,0:T(8,128)(2,1)}, s32[]{:T(128)}, ...), condition=%wide.region_5.6_spmd.clone, body=%wide.region_4.5_spmd.clone.sunk | while | flops 1048584 | bytes 2621595 | solution.py:36
  573.7 1.7 add_select_fusion.5
  626.4 3.1 fusion.2
  629.5 2.0 copy.50
  631.5 3.4 convolution_add_fusion.1
  (118 shorter events, 116.6 us)
Async XLA Ops:
  7.2 267.8 %copy-start = (bf16[1,128,2048]{2,1,0:T(8,128)(2,1)S(1)}, bf16[1,128,2048]{2,1,0:T(8,128)(2,1)}, u32[]{:S(2)}) copy-start(bf16[1,128,2048]{2,1,0:T(8,128)(2,1)} %param.15) | copy-start | bytes 1572868
  7.2 193.3 %all-gather.10.cloned.1.call-start = ((), (), s32[]{:S(2)}) async-start(), calls=%async_computation.3 | async-start | bytes 34603008 | tf_op jit(solution)/shard_map/all_gather | solution.py:14
  8.7 191.7 %copy-start.8 = (bf16[16,8,16,128]{3,2,1,0:T(8,128)(2,1)}, bf16[16,8,16,128]{3,2,1,0:T(8,128)(2,1)S(1)}, u32[]{:S(2)}) copy-start(bf16[16,8,16,128]{3,2,1,0:T(8,128)(2,1)S(1)} %copy.57) | copy-start | bytes 1572868
  9.2 3.5 copy-start.10
  10.6 243.1 %copy-start.5 = (bf16[16,8,16,128]{3,2,1,0:T(8,128)(2,1)}, bf16[16,8,16,128]{3,2,1,0:T(8,128)(2,1)S(1)}, u32[]{:S(2)}) copy-start(bf16[16,8,16,128]{3,2,1,0:T(8,128)(2,1)S(1)} %copy.58) | copy-start | bytes 1572868
  11.9 263.1 %all-gather.8.cloned.1.call-start = ((), (), s32[]{:S(2)}) async-start(), calls=%async_computation.1 | async-start | bytes 8650752 | tf_op jit(solution)/shard_map/all_gather | solution.py:62
  12.6 399.8 %reduce-scatter.2.cloned.1.call-start = ((), (), s32[]{:S(2)}) async-start(), calls=%async_computation.2 | async-start | bytes 8650752 | tf_op jit(solution)/shard_map/reduce_scatter | solution.py:143
  16.1 236.6 %copy-start.2 = (bf16[1,128,2048]{1,2,0:T(8,128)(2,1)}, bf16[1,128,2048]{1,2,0:T(8,128)(2,1)S(1)}, u32[]{:S(2)}) copy-start(bf16[1,128,2048]{1,2,0:T(8,128)(2,1)S(1)} %copy.56) | copy-start | bytes 1572868
  200.4 74.6 %copy-start.13 = (f32[2048]{0:T(1024)S(1)}, f32[2048]{0:T(1024)}, u32[]{:S(2)}) copy-start(f32[2048]{0:T(1024)} %param.13) | copy-start | bytes 24580
  281.9 130.8 %copy-start.3 = (bf16[1,128,2048]{1,2,0:T(8,128)(2,1)S(1)}, bf16[1,128,2048]{1,2,0:T(8,128)(2,1)}, u32[]{:S(2)}) copy-start(bf16[1,128,2048]{1,2,0:T(8,128)(2,1)} %copy-done.2) | copy-start | bytes 1572868
  281.9 130.8 %copy-start.7 = (bf16[128,16,128]{0,2,1:T(8,128)(2,1)S(1)}, bf16[128,16,128]{0,2,1:T(8,128)(2,1)}, u32[]{:S(2)}) copy-start(bf16[128,16,128]{0,2,1:T(8,128)(2,1)} %get-tuple-element.254) | copy-start | bytes 1572868
  287.5 136.6 %copy-start.4 = (bf16[1,128,2048]{1,2,0:T(8,128)(2,1)S(1)}, bf16[1,128,2048]{1,2,0:T(8,128)(2,1)}, u32[]{:S(2)}) copy-start(bf16[1,128,2048]{1,2,0:T(8,128)(2,1)} %copy-done.2) | copy-start | bytes 1572868
  287.6 185.9 %all-gather.14.cloned.1.call-start = ((), (), s32[]{:S(2)}) async-start(), calls=%async_computation.5 | async-start | bytes 2359296 | tf_op jit(solution)/shard_map/all_gather | solution.py:56
  412.5 161.2 %all-gather.12.cloned.1.call-start = ((), (), s32[]{:S(2)}) async-start(), calls=%async_computation.4 | async-start | bytes 17301504 | tf_op jit(solution)/shard_map/all_gather | solution.py:27
  415.7 4.4 copy-start.12
  434.1 192.3 %copy-start.9 = (bf16[16,8,16,128]{3,2,1,0:T(8,128)(2,1)S(1)}, bf16[16,8,16,128]{3,2,1,0:T(8,128)(2,1)}, u32[]{:S(2)}) copy-start(bf16[16,8,16,128]{3,2,1,0:T(8,128)(2,1)} %copy-done.8) | copy-start | bytes 1572868
  573.6 57.9 %copy-start.6 = (bf16[16,8,16,128]{3,2,1,0:T(8,128)(2,1)S(1)}, bf16[16,8,16,128]{3,2,1,0:T(8,128)(2,1)}, u32[]{:S(2)}) copy-start(bf16[16,8,16,128]{3,2,1,0:T(8,128)(2,1)} %copy-done.5) | copy-start | bytes 1572868
  573.6 62.9 %copy-start.11 = (bf16[1,128,2048]{2,1,0:T(8,128)(2,1)S(1)}, bf16[1,128,2048]{2,1,0:T(8,128)(2,1)}, u32[]{:S(2)}) copy-start(bf16[1,128,2048]{2,1,0:T(8,128)(2,1)} %param.11) | copy-start | bytes 1572868
  626.4 11.2 %copy-start.1 = (bf16[1,128,2048]{2,1,0:T(8,128)(2,1)S(1)}, bf16[1,128,2048]{2,1,0:T(8,128)(2,1)}, u32[]{:S(2)}) copy-start(bf16[1,128,2048]{2,1,0:T(8,128)(2,1)} %param.15) | copy-start | bytes 1572868
Sparse Core Ops, SparseCore 0:
  12.0 188.4 all-gather.9
  202.3 72.6 all-gather.7
  287.7 124.7 reduce-scatter.1
  414.9 58.4 all-gather.13
  475.1 98.4 all-gather.11
